TPU v7x, 32 devices: a whole 2x2x4 slice. The times are simulated.
32 devices in a mesh: lat: 4 (over z), lon: 8 (over y, x, core).
Axes of the slice: x: 2, y: 2, z: 4, core: 2. Of those that a mesh axis runs over, the one named last changes fastest.
Arguments:
- fields: float32 [5, 960, 2880], P(None, 'lat', 'lon'), may hold values from -6 to 6
- east_courant: float32 [960, 2880], P('lat', 'lon'), may hold values from -0.4 to 0.4
- north_courant: float32 [960, 2880], P('lat', 'lon'), may hold values from -0.4 to 0.4
- cutoff: int32 [960], replicated, may hold values from 1 to 1439
- damping: float32 [960], replicated, may hold values from 0.05 to 0.5
- ship_rows: int32 [4, 4, 60], replicated, may hold values from -1 to 239, as said below
Outputs:
- updated: float32 [5, 960, 2880], P(None, 'lat', 'lon')
Inputs may be any that keep to these rules, and one draw needn't show every extreme that they name: ship_rows[s, d, j] is a row of band s (0 to 239) whose filter is computed by band d, or -1 for an empty slot; no row is listed twice; every row within 240 rows of either pole is listed, no row farther than 360 from both poles is listed, and rows between are listed or not, so that bands 0 and 3 are covered whole; a band's listed rows fill the slots of its destinations in full except the last destination it uses, so band 0 fills 60 slots to some band.
All inputs are finite; a program needn't handle non-finite values.
Results may differ from a plain program's by a relative error of at most 0.0003.
Values sent between devices are 32-bit elements; how exact they have to be, the bound alone decides.
A program may use at most 256 MiB of HBM per device.

v0:
```python
import math
import jax
import jax.numpy as jnp
from jax import lax
from jax.sharding import PartitionSpec as P

HIGHEST_PRECISION = lax.Precision.HIGHEST


def with_halo(cells, sides, width, closed):
    for axis, dim in sides:
        count = lax.axis_size(axis)
        ends = count if closed else count - 1
        head = lax.slice_in_dim(cells, 0, width, axis=dim)
        tail = lax.slice_in_dim(cells, cells.shape[dim] - width, cells.shape[dim], axis=dim)
        cells = jnp.concatenate(
            [
                lax.ppermute(tail, axis, [(i, (i + 1) % count) for i in range(ends)]),
                cells,
                lax.ppermute(head, axis, [((i + 1) % count, i) for i in range(ends)]),
            ],
            axis=dim,
        )
    return cells


def phase_pair(cutoffs, positions, length):
    turned = (2 * cutoffs[:, None] + 1) * positions[None, :] % (2 * length)
    angles = turned.astype(jnp.float32) * (math.pi / length)
    return (jnp.cos(angles), jnp.sin(angles))


def kernel_block(sources, targets, length):
    offsets = targets[None, :] - sources[:, None]
    magnitude = jnp.abs(offsets)
    nearest = jnp.minimum(magnitude, length - magnitude)
    nonzero = jnp.where(nearest == 0, 1, nearest)
    values = jnp.sign(offsets).astype(jnp.float32) / (
        length * jnp.sin(nonzero.astype(jnp.float32) * (math.pi / length))
    )
    return jnp.where(offsets == 0, jnp.float32(0.0), values)


def modulated_sum(running, column_piece, cutoffs, targets, length):
    piece_count = column_piece.shape[2]
    sources = jnp.arange(piece_count, dtype=jnp.int32)
    cos_part, sin_part = phase_pair(cutoffs, sources, length)
    stacked = jnp.stack([column_piece * cos_part[:, None, :], column_piece * sin_part[:, None, :]])
    flattened = stacked.reshape(-1, piece_count)
    kernel = kernel_block(sources, targets, length)
    product = jnp.dot(
        flattened, kernel, precision=HIGHEST_PRECISION, preferred_element_type=jnp.float32
    )
    return product.reshape(running.shape)


def finish_filter(running, local_rows, cutoffs, targets, damping_rows, length):
    cos_part, sin_part = phase_pair(cutoffs, targets, length)
    centre = (2 * cutoffs + 1).astype(jnp.float32) / length
    lowpass = (
        sin_part[:, None, :] * running[0]
        - cos_part[:, None, :] * running[1]
        + centre[:, None, None] * local_rows
    )
    return damping_rows[:, None, None] * local_rows + (1.0 - damping_rows[:, None, None]) * lowpass


def table_lookup(lookup_table, indices):
    matches = indices[:, None] == jnp.arange(lookup_table.shape[0], dtype=jnp.int32)[None, :]
    return jnp.sum(
        jnp.where(matches, lookup_table[None, :], jnp.zeros_like(lookup_table)[None, :]), axis=1
    )


def per_device(fields, east_courant, north_courant, cutoff, damping, ship_rows):
    channel_count, rows_dev, cols_dev = fields.shape
    band_count = lax.axis_size("lat")
    segment_count = lax.axis_size("lon")
    lat_count = rows_dev * band_count
    lon_count = cols_dev * segment_count
    band_index = lax.axis_index("lat")
    segment_index = lax.axis_index("lon")
    zonal = with_halo(jnp.concatenate([fields, east_courant[None]], axis=0), (("lon", 2),), 1, True)
    meridional = with_halo(
        jnp.concatenate([fields, north_courant[None]], axis=0), (("lat", 1),), 1, False
    )
    east_cells = zonal[:channel_count, :, 2:]
    west_cells = zonal[:channel_count, :, :-2]
    west_courant = zonal[channel_count, :, :-2]
    east_flux = east_courant * jnp.where(east_courant > 0, fields, east_cells)
    west_flux = west_courant * jnp.where(west_courant > 0, west_cells, fields)
    global_rows = band_index * rows_dev + jnp.arange(rows_dev, dtype=jnp.int32)
    latitudes = global_rows.astype(jnp.float32)
    face_n = jnp.sin((latitudes + 1.0) * (math.pi / lat_count))
    face_s = jnp.sin(latitudes * (math.pi / lat_count))
    centre = jnp.sin((latitudes + 0.5) * (math.pi / lat_count))
    north_mask = (global_rows < lat_count - 1).astype(jnp.float32)
    south_mask = (global_rows > 0).astype(jnp.float32)
    north_cells = meridional[:channel_count, 2:, :]
    south_cells = meridional[:channel_count, :-2, :]
    south_courant = meridional[channel_count, :-2, :]
    north_flux = (
        north_courant
        * jnp.where(north_courant > 0, fields, north_cells)
        * (face_n * north_mask)[:, None]
    )
    south_flux = (
        south_courant
        * jnp.where(south_courant > 0, south_cells, fields)
        * (face_s * south_mask)[:, None]
    )
    advected = fields - (east_flux - west_flux) - (north_flux - south_flux) / centre[:, None]
    outgoing_rows = lax.dynamic_index_in_dim(ship_rows, band_index, axis=0, keepdims=False).reshape(
        -1
    )
    outgoing_valid = outgoing_rows >= 0
    picked = jnp.take(advected, jnp.maximum(outgoing_rows, 0), axis=1)
    picked = jnp.where(outgoing_valid[None, :, None], picked, jnp.float32(0.0)).transpose(1, 0, 2)
    slot_count = picked.shape[0]
    arrived = lax.all_to_all(
        picked.reshape(band_count, -1, channel_count, cols_dev),
        "lat",
        split_axis=0,
        concat_axis=0,
        tiled=True,
    )
    arrived = arrived.reshape(slot_count, channel_count, cols_dev)
    incoming_rows = lax.dynamic_index_in_dim(ship_rows, band_index, axis=1, keepdims=False).reshape(
        -1
    )
    capacity = slot_count // band_count
    source_band = jnp.arange(slot_count, dtype=jnp.int32) // capacity
    incoming_global = jnp.where(incoming_rows >= 0, source_band * rows_dev + incoming_rows, 0)
    cutoffs = table_lookup(cutoff, incoming_global)
    damping_rows = table_lookup(damping, incoming_global)
    targets = segment_index * cols_dev + jnp.arange(cols_dev, dtype=jnp.int32)
    initial = jnp.zeros((2,) + arrived.shape, jnp.float32)
    running = modulated_sum(
        initial, lax.all_gather(arrived, "lon", axis=2, tiled=True), cutoffs, targets, lon_count
    )
    filtered = finish_filter(running, arrived, cutoffs, targets, damping_rows, lon_count)
    returned = lax.all_to_all(
        filtered.reshape(band_count, -1, channel_count, cols_dev),
        "lat",
        split_axis=0,
        concat_axis=0,
        tiled=True,
    )
    returned = returned.reshape(slot_count, channel_count, cols_dev)
    placement = jnp.where(outgoing_valid, outgoing_rows, rows_dev)
    return advected.at[:, placement, :].set(returned.transpose(1, 0, 2), mode="drop")


def solution(mesh):
    placed = (P(None, "lat", "lon"), P("lat", "lon"), P("lat", "lon"), P(), P(), P())
    return jax.shard_map(
        per_device, mesh=mesh, in_specs=placed, out_specs=P(None, "lat", "lon"), check_vma=False
    )
```

profile of v0, /device:TPU:0, one launch (start us, length us, event | category | flops | bytes accessed | tf_op | source)
XLA Modules:
  0.0 518.8 jit_solution(7479676274369579383)
XLA Ops:
  6.5 2.3 copy.66
  9.2 0.6 pad_maximum_fusion.13
  9.8 4.9 collective-permute-start.3
  14.7 1.3 collective-permute-start.2
  16.0 1.3 pad_maximum_fusion.10
  17.4 2.0 copy.63
  19.4 1.4 copy.61
  20.7 2.7 collective-permute-start
  23.5 1.0 broadcast_compare_fusion.1
  24.5 1.3 maximum_compare_fusion
  25.8 0.6 reshape.267
  27.0 0.6 compare_select_fusion.4
  27.6 1.3 broadcast_maximum_fusion
  28.9 0.6 multiply_sine_fusion
  29.5 1.3 ge.36
  30.8 1.2 le.16
  32.0 1.8 copy.64
  33.8 1.8 maximum_bitcast_fusion
  35.6 1.7 fusion.52
  37.3 1.9 copy.62
  39.2 4.4 fusion.42
  43.6 0.7 pad_maximum_fusion.11
  44.6 5.1 fusion.23
  49.7 2.6 gather_fusion
  52.3 1.3 select_select_fusion
  54.0 50.3 %all_to_all.10 = f32[4,60,5,360]{3,1,2,0:T(8,128)S(1)} all-to-all(f32[4,60,5,360]{3,1,2,0:T(8,128)S(1)} %copy.69), channel_id=1, replica_groups=mesh['lat'=4,'lon'=8] {'lat'}, dimensions={0} | all-to-all | bytes 3456000 | tf_op jit(solution)/shard_map/all_to_all | solution.py:120
  104.3 3.6 copy.81
  107.9 5.2 %reshape.289 = f32[240,5,360]{0,1,2:T(8,128)} reshape(f32[4,60,5,360]{1,0,2,3:T(4,128)} %copy.81) | data formatting | bytes 3456000 | tf_op jit(solution)/shard_map/reshape | solution.py:127
  113.2 0.7 dynamic-slice_reduce_fusion
  114.7 1.7 fusion.50
  116.4 13.7 %fusion.30 = (f32[240,2880]{0,1:T(8,128)}, f32[240,2880]{0,1:T(8,128)}) fusion(s32[240]{0:T(256)S(1)} %multiply_add_fusion), kind=kLoop, calls=%fused_computation.45 | loop fusion | flops 6220800 | bytes 5530560 | tf_op jit(solution)/shard_map/cos | solution.py:30
  130.1 18.3 %fusion.66 = f32[2880,360]{1,0:T(8,128)} fusion(s32[360]{0:T(512)S(1)} %iota_add_fusion), kind=kLoop, calls=%fused_computation.12.clone.clone.1 | loop fusion | flops 14515200 | bytes 4148640 | tf_op jit(solution)/shard_map/dot_general | solution.py:51
  148.4 81.8 %all-gather.2.cloned.1.call-done = f32[240,5,2880]{0,1,2:T(8,128)} async-done(((f32[240,5,360]{0,1,2:T(8,128)}), f32[240,5,2880]{0,1,2:T(8,128)}) %all-gather.2.cloned.1.call-update) | async-done | bytes 13824016 | tf_op jit(solution)/shard_map/all_gather | solution.py:139
  230.1 26.0 %multiply_bitcast_fusion.1 = (f32[1,240,5,2880]{1,2,3,0:T(8,128)}, f32[1,240,5,2880]{1,2,3,0:T(8,128)}) fusion(f32[240,5,2880]{0,1,2:T(8,128)} %all-gather.2.cloned.1.call-done, f32[240,2880]{0,1:T(8,128)} %get-tuple-element.17, f32[240,2880]{0,1:T(8,128)} %get-tuple-element.18), kind=kLoop, calls=%fused_computation.4 | loop fusion | flops 6912000 | bytes 47001600 | tf_op jit(solution)/shard_map/stack | solution.py:48
  256.1 34.0 %pad_maximum_fusion = f32[2,240,5,2880]{1,2,3,0:T(8,128)} fusion(f32[1,240,5,2880]{1,2,3,0:T(8,128)} %get-tuple-element.8, f32[1,240,5,2880]{1,2,3,0:T(8,128)} %get-tuple-element.7), kind=kLoop, calls=%fused_computation.2 | loop fusion | flops 6912000 | bytes 55296000 | tf_op jit(solution)/shard_map/stack | solution.py:48
  290.1 47.7 %copy.73 = f32[2,240,5,2880]{3,2,1,0:T(8,128)} copy(f32[2,240,5,2880]{1,2,3,0:T(8,128)} %pad_maximum_fusion) | data formatting | bytes 55296000 | tf_op jit(solution)/shard_map/stack | solution.py:48
  337.8 35.2 %reshape.271 = f32[2400,2880]{1,0:T(8,128)} reshape(f32[2,240,5,2880]{3,2,1,0:T(8,128)} %copy.73) | data formatting | bytes 55296000 | tf_op jit(solution)/shard_map/reshape | solution.py:49
  373.0 43.7 %fusion.6 = f32[2400,360]{0,1:T(8,128)S(1)} fusion(f32[2400,2880]{1,0:T(8,128)} %reshape.271, f32[2880,360]{1,0:T(8,128)} %fusion.66), kind=kOutput, calls=%fused_computation.13 | convolution fusion | flops 29859840000 | bytes 35251200 | tf_op jit(solution)/shard_map/dot_general | solution.py:51
  416.7 2.4 fusion.61
  419.2 2.8 copy.75
  422.0 3.1 squeeze.13
  425.1 2.8 copy.74
  427.8 3.1 squeeze.12
  430.9 4.7 fusion.13
  436.0 50.2 %all_to_all.11 = f32[4,60,5,360]{3,1,2,0:T(8,128)S(1)} all-to-all(f32[4,60,5,360]{3,1,2,0:T(8,128)S(1)} %copy.77), channel_id=1, replica_groups=mesh['lat'=4,'lon'=8] {'lat'}, dimensions={0} | all-to-all | bytes 3456000 | tf_op jit(solution)/shard_map/all_to_all | solution.py:142
  486.2 2.7 copy.82
  488.9 21.5 %scatter_fusion = f32[5,240,360]{2,0,1:T(8,128)S(1)} fusion(f32[5,240,360]{2,0,1:T(8,128)S(1)} %copy-done, s32[240]{0:T(256)S(1)} %bitcast.30, f32[240,5,360]{2,1,0:T(8,128)} %bitcast.28), kind=kCustom, calls=%fused_computation.1 | custom fusion | bytes 5184960 | tf_op jit(solution)/shard_map/scatter | solution.py:151
  510.4 1.6 copy.80
  (54 shorter events, 2.6 us)
Async XLA Ops:
  6.5 223.6 %all-gather.2.cloned.1.call-start = ((), (), s32[]{:S(2)}) async-start(), calls=%async_computation.2 | async-start | bytes 26542080 | tf_op jit(solution)/shard_map/all_gather | solution.py:139
  6.5 2.3 copy-start.5
  8.9 7.2 %copy-start.1 = (f32[5,240,360]{2,1,0:T(8,128)S(1)}, f32[5,240,360]{2,1,0:T(8,128)}, u32[]{:S(2)}) copy-start(f32[5,240,360]{2,1,0:T(8,128)} %param.6) | copy-start | bytes 5184004
  8.9 7.2 %copy-start.2 = (f32[240,360]{1,0:T(8,128)S(1)}, f32[240,360]{1,0:T(8,128)}, u32[]{:S(2)}) copy-start(f32[240,360]{1,0:T(8,128)} %param.7) | copy-start | bytes 1036804
  9.1 8.2 %copy-start.3 = (f32[1,240,360]{2,0,1:T(1,128)}, f32[1,240,360]{2,0,1:T(1,128)S(1)}, u32[]{:S(2)}) copy-start(f32[1,240,360]{2,0,1:T(1,128)S(1)} %broadcast_in_dim.115) | copy-start | bytes 1036804
  9.8 33.8 %collective-permute-start.3 = (f32[6,1,360]{2,0,1:T(8,128)}, f32[6,1,360]{2,0,1:T(8,128)S(1)}, u32[]{:S(2)}, u32[]{:S(2)}) collective-permute-start(f32[6,1,360]{2,0,1:T(8,128)} %get-tuple-element.12), channel_id=1, source_target_pairs={{0,8},{8,16},{16,24},{1,9},{9,17},{17,25},{2,10},{10,18},{18,26},{... | collective-permute-start | bytes 25928 | tf_op jit(solution)/shard_map/ppermute | solution.py:18
  14.7 29.7 %collective-permute-start.2 = (f32[6,1,360]{2,0,1:T(8,128)S(1)}, f32[6,1,360]{2,0,1:T(8,128)S(1)}, u32[]{:S(2)}, u32[]{:S(2)}) collective-permute-start(f32[6,1,360]{2,0,1:T(8,128)S(1)} %get-tuple-element.11), channel_id=1, source_target_pairs={{8,0},{16,8},{24,16},{9,1},{17,9},{25,17},{10,2},{18,10},{26,18},{... | collective-permute-start | bytes 25928 | tf_op jit(solution)/shard_map/ppermute | solution.py:20
  19.4 12.6 %collective-permute-start.1 = (f32[6,240,1]{1,2,0:T(1,128)}, f32[6,240,1]{1,2,0:T(1,128)}, u32[]{:S(2)}, u32[]{:S(2)}) collective-permute-start(f32[6,240,1]{1,2,0:T(1,128)} %copy.63), channel_id=1, source_target_pairs={{0,1},{1,2},{2,3},{3,4},{4,5},{5,6},{6,7},{7,0},{8,9},{9,10},{10,1... | collective-permute-start | bytes 17288 | tf_op jit(solution)/shard_map/ppermute | solution.py:18
  20.7 16.6 %collective-permute-start = (f32[6,240,1]{1,2,0:T(1,128)S(1)}, f32[6,240,1]{1,2,0:T(1,128)}, u32[]{:S(2)}, u32[]{:S(2)}) collective-permute-start(f32[6,240,1]{1,2,0:T(1,128)S(1)} %copy.61), channel_id=1, source_target_pairs={{1,0},{2,1},{3,2},{4,3},{5,4},{6,5},{7,6},{0,7},{9,8},{10,9},{11,1... | collective-permute-start | bytes 17288 | tf_op jit(solution)/shard_map/ppermute | solution.py:20
  39.2 4.4 copy-start.4
  43.6 1.0 copy-start.6
  43.6 1.0 copy-start.8
  43.6 1.0 copy-start.9
  43.6 1.0 copy-start.12
  49.7 2.6 copy-start.13
  49.7 2.6 copy-start.14
  113.1 0.9 copy-start.10
  113.1 1.2 copy-start.11
  486.2 2.7 copy-start
  486.2 2.7 copy-start.7
Sparse Core Ops, SparseCore 0:
  113.3 116.7 all-gather.1
where the time goes:
time: 522 us; the launch traced here: 519 us
  local copies, waits for them, and re-layouts  149 us (29%)
  other arithmetic  121 us (23%)
  blocking collectives  100 us (19%)
  waiting for transfers between devices  81.8 us (16%)
  matrix products  43.7 us (8%)
  between operations  13.7 us (3%)
  starting transfers between devices  8.91 us (2%)
    all_gather x1, waiting for transfers between devices, per_device(): lax.all_gather(arrived, 'lon', axis=2, tiled=True)  81.8 us
    another operation x2, other arithmetic, modulated_sum(): jnp.stack([column_piece * cos_part[:, None, :], column_piece * sin_part[:...  60 us
    all_to_all x1, blocking collectives, per_device(): lax.all_to_all(picked.reshape(band_count, -1, channel_count, cols_dev), '...  50.3 us
    all_to_all x1, blocking collectives, per_device(): lax.all_to_all(filtered.reshape(band_count, -1, channel_count, cols_dev),...  50.2 us
    another operation x1, local copies, waits for them, and re-layouts, modulated_sum(): jnp.stack([column_piece * cos_part[:, None, :], column_piece * sin_part[:...  47.7 us
    dot_general x1, matrix products, modulated_sum(): jnp.dot(flattened, kernel, precision=HIGHEST_PRECISION, preferred_element...  43.7 us
    reshape x1, local copies, waits for them, and re-layouts, modulated_sum(): flattened = stacked.reshape(-1, piece_count)  35.2 us
    scatter x2, local copies, waits for them, and re-layouts, per_device(): advected.at[:, placement, :].set(returned.transpose(1, 0, 2), mode='drop')  23 us
  transfers between devices with their start and end apart: 5, of which 1 were waited for; matrix products, arithmetic and copies ran while one was open for 12% of the time, Pallas kernels for 0%

commit v1 on v0

--- a/solution.py
+++ b/solution.py
@@ -5,6 +5,19 @@
 from jax.sharding import PartitionSpec as P
 
 HIGHEST_PRECISION = lax.Precision.HIGHEST
+
+
+def gather_around(x, axis, dim):
+    devices, index, rows = (lax.axis_size(axis), lax.axis_index(axis), x.shape[dim])
+    forward = [(i, (i + 1) % devices) for i in range(devices)]
+    out = jnp.zeros((*x.shape[:dim], devices * rows, *x.shape[dim + 1 :]), x.dtype)
+    block = x
+    for turn in range(devices):
+        source = (index - turn) % devices
+        out = lax.dynamic_update_slice_in_dim(out, block, source * rows, axis=dim)
+        if turn < devices - 1:
+            block = lax.ppermute(block, axis, forward)
+    return out
 
 
 def with_halo(cells, sides, width, closed):
@@ -135,9 +148,7 @@
     damping_rows = table_lookup(damping, incoming_global)
     targets = segment_index * cols_dev + jnp.arange(cols_dev, dtype=jnp.int32)
     initial = jnp.zeros((2,) + arrived.shape, jnp.float32)
-    running = modulated_sum(
-        initial, lax.all_gather(arrived, "lon", axis=2, tiled=True), cutoffs, targets, lon_count
-    )
+    running = modulated_sum(initial, gather_around(arrived, "lon", 2), cutoffs, targets, lon_count)
     filtered = finish_filter(running, arrived, cutoffs, targets, damping_rows, lon_count)
     returned = lax.all_to_all(
         filtered.reshape(band_count, -1, channel_count, cols_dev),

time: 522 us -> 870 us (1.67)
  local copies, waits for them, and re-layouts: 149 us -> 451 us
  waiting for transfers between devices: 81.8 us -> 139 us
  between operations: 13.7 us -> 0.83 us
    dynamic_update_slice x0 -> x8, local copies, waits for them, and re-layouts: none -> 311 us  [gather_around(): out = lax.dynamic_update_slice_in_dim(out, block, source * rows, axis=dim)]
    ppermute x0 -> x7, waiting for transfers between devices: none -> 139 us  [gather_around(): block = lax.ppermute(block, axis, forward)]
    all_gather x1 -> x0, waiting for transfers between devices: 81.8 us -> none  [per_device(): lax.all_gather(arrived, 'lon', axis=2, tiled=True)]
    another operation x1 -> x0, local copies, waits for them, and re-layouts: 47.7 us -> none  [modulated_sum(): jnp.stack([column_piece * cos_part[:, None, :], column_piece * sin_part[:...]
    ppermute x0 -> x7, local copies, waits for them, and re-layouts: none -> 27 us  [gather_around(): block = lax.ppermute(block, axis, forward)]
    broadcast_in_dim x0 -> x1, local copies, waits for them, and re-layouts: none -> 8.97 us  [gather_around(): jnp.zeros((*x.shape[:dim], devices * rows, *x.shape[dim + 1:]), x.dtype)]
  transfers between devices with their start and end apart: 5 -> 11, of which waited for: 1 -> 6; matrix products, arithmetic and copies ran while one was open for 12% -> 43% of each run, Pallas kernels for 0% -> 0%
where the time goes in v1:
time: 870 us; the launch traced here: 858 us
  local copies, waits for them, and re-layouts  451 us (52%)
  waiting for transfers between devices  139 us (16%)
  other arithmetic  120 us (14%)
  blocking collectives  94.6 us (11%)
  matrix products  43.7 us (5%)
  starting transfers between devices  9.08 us (1%)
    dynamic_update_slice x8, local copies, waits for them, and re-layouts, gather_around(): out = lax.dynamic_update_slice_in_dim(out, block, source * rows, axis=dim)  311 us
    ppermute x7, waiting for transfers between devices, gather_around(): block = lax.ppermute(block, axis, forward)  139 us
    another operation x2, other arithmetic, modulated_sum(): jnp.stack([column_piece * cos_part[:, None, :], column_piece * sin_part[:...  57.8 us
    all_to_all x1, blocking collectives, per_device(): lax.all_to_all(picked.reshape(band_count, -1, channel_count, cols_dev), '...  50.3 us
    all_to_all x1, blocking collectives, per_device(): lax.all_to_all(filtered.reshape(band_count, -1, channel_count, cols_dev),...  44.3 us
    dot_general x1, matrix products, modulated_sum(): jnp.dot(flattened, kernel, precision=HIGHEST_PRECISION, preferred_element...  43.7 us
    reshape x1, local copies, waits for them, and re-layouts, modulated_sum(): flattened = stacked.reshape(-1, piece_count)  35.2 us
    ppermute x7, local copies, waits for them, and re-layouts, gather_around(): block = lax.ppermute(block, axis, forward)  27 us
  transfers between devices with their start and end apart: 11, of which 6 were waited for; matrix products, arithmetic and copies ran while one was open for 43% of the time, Pallas kernels for 0%

profile of v1, /device:TPU:0, one launch (start us, length us, event | category | flops | bytes accessed | tf_op | source)
XLA Modules:
  0.0 858.2 jit_solution(7588310639317248430)
XLA Ops:
  0.0 2.3 copy.85
  3.2 4.9 collective-permute-start.3
  10.8 2.0 copy.82
  14.2 2.7 collective-permute-start
  30.8 1.8 copy.81
  32.6 4.3 fusion.42
  38.0 5.1 fusion.21
  43.1 2.6 gather_fusion
  47.4 50.3 %all_to_all.10 = f32[4,60,5,360]{3,1,2,0:T(8,128)S(1)} all-to-all(f32[4,60,5,360]{3,1,2,0:T(8,128)S(1)} %copy.88), channel_id=1, replica_groups=mesh['lat'=4,'lon'=8] {'lat'}, dimensions={0} | all-to-all | bytes 3456000 | tf_op jit(solution)/shard_map/all_to_all | solution.py:133
  99.1 2.6 reshape.270
  101.7 23.8 %collective-permute-done.4 = f32[240,5,360]{2,0,1:T(8,128)S(1)} collective-permute-done((f32[240,5,360]{2,0,1:T(8,128)}, f32[240,5,360]{2,0,1:T(8,128)S(1)}, u32[]{:S(2)}, u32[]{:S(2)}) %collective-permute-start.4) | collective-permute-done | bytes 1728032 | tf_op jit(solution)/shard_map/ppermute | solution.py:19
  126.9 23.6 %collective-permute-done.5 = f32[240,5,360]{2,0,1:T(8,128)S(1)} collective-permute-done((f32[240,5,360]{2,0,1:T(8,128)S(1)}, f32[240,5,360]{2,0,1:T(8,128)S(1)}, u32[]{:S(2)}, u32[]{:S(2)}) %collective-permute-start.5) | collective-permute-done | bytes 1728032 | tf_op jit(solution)/shard_map/ppermute | solution.py:19
  151.8 23.6 %collective-permute-done.6 = f32[240,5,360]{2,0,1:T(8,128)S(1)} collective-permute-done((f32[240,5,360]{2,0,1:T(8,128)S(1)}, f32[240,5,360]{2,0,1:T(8,128)S(1)}, u32[]{:S(2)}, u32[]{:S(2)}) %collective-permute-start.6) | collective-permute-done | bytes 1728032 | tf_op jit(solution)/shard_map/ppermute | solution.py:19
  176.7 23.6 %collective-permute-done.7 = f32[240,5,360]{2,0,1:T(8,128)S(1)} collective-permute-done((f32[240,5,360]{2,0,1:T(8,128)S(1)}, f32[240,5,360]{2,0,1:T(8,128)S(1)}, u32[]{:S(2)}, u32[]{:S(2)}) %collective-permute-start.7) | collective-permute-done | bytes 1728032 | tf_op jit(solution)/shard_map/ppermute | solution.py:19
  201.5 23.7 %collective-permute-done.8 = f32[240,5,360]{2,0,1:T(8,128)} collective-permute-done((f32[240,5,360]{2,0,1:T(8,128)S(1)}, f32[240,5,360]{2,0,1:T(8,128)}, u32[]{:S(2)}, u32[]{:S(2)}) %collective-permute-start.8) | collective-permute-done | bytes 1728032 | tf_op jit(solution)/shard_map/ppermute | solution.py:19
  228.5 20.7 %collective-permute-done.9 = f32[240,5,360]{2,0,1:T(8,128)} collective-permute-done((f32[240,5,360]{2,0,1:T(8,128)}, f32[240,5,360]{2,0,1:T(8,128)}, u32[]{:S(2)}, u32[]{:S(2)}) %collective-permute-start.9) | collective-permute-done | bytes 1728032 | tf_op jit(solution)/shard_map/ppermute | solution.py:19
  249.4 14.0 %fusion.30 = (f32[240,2880]{1,0:T(8,128)}, f32[240,2880]{1,0:T(8,128)}) fusion(s32[240]{0:T(256)S(1)} %multiply_add_fusion), kind=kLoop, calls=%fused_computation.45 | loop fusion | flops 6220800 | bytes 5530560 | tf_op jit(solution)/shard_map/cos | solution.py:43
  263.5 18.3 %fusion.66 = f32[2880,360]{1,0:T(8,128)} fusion(s32[360]{0:T(512)S(1)} %iota_add_fusion), kind=kLoop, calls=%fused_computation.12.clone.clone.1 | loop fusion | flops 14515200 | bytes 4148640 | tf_op jit(solution)/shard_map/dot_general | solution.py:64
  281.8 2.4 copy.91
  284.1 9.0 %broadcast_in_dim.130 = f32[240,5,2880]{2,1,0:T(8,128)} broadcast(f32[]{:T(128)} %constant.133.clone.1), dimensions={} | broadcast | bytes 13824004 | tf_op jit(solution)/shard_map/broadcast_in_dim | solution.py:13
  293.1 16.7 %dynamic_update_slice.24 = f32[240,5,2880]{2,1,0:T(8,128)} dynamic-update-slice(f32[240,5,2880]{2,1,0:T(8,128)} %broadcast_in_dim.130, f32[240,5,360]{2,1,0:T(8,128)} %copy.91, s32[]{:T(128)} %constant.139.clone.1, s32[]{:T(128)} %constant.139.clone.1, s32[]{:T(128)S(6)} %select_n.189) | dynamic-update-slice | bytes 3456004 | tf_op jit(solution)/shard_map/dynamic_update_slice | solution.py:17
  309.8 3.9 copy.92
  313.7 42.0 %dynamic_update_slice.25 = f32[240,5,2880]{2,1,0:T(8,128)} dynamic-update-slice(f32[240,5,2880]{2,1,0:T(8,128)} %dynamic_update_slice.24, f32[240,5,360]{2,1,0:T(8,128)} %copy.92, s32[]{:T(128)} %constant.139.clone.1, s32[]{:T(128)} %constant.139.clone.1, s32[]{:T(128)S(6)} %select_n.191) | dynamic-update-slice | bytes 3456004 | tf_op jit(solution)/shard_map/dynamic_update_slice | solution.py:17
  355.7 3.9 copy.93
  359.5 42.1 %dynamic_update_slice.26 = f32[240,5,2880]{2,1,0:T(8,128)} dynamic-update-slice(f32[240,5,2880]{2,1,0:T(8,128)} %dynamic_update_slice.25, f32[240,5,360]{2,1,0:T(8,128)} %copy.93, s32[]{:T(128)} %constant.139.clone.1, s32[]{:T(128)} %constant.139.clone.1, s32[]{:T(128)S(6)} %select_n.193) | dynamic-update-slice | bytes 3456004 | tf_op jit(solution)/shard_map/dynamic_update_slice | solution.py:17
  401.6 3.9 copy.94
  405.5 42.1 %dynamic_update_slice.27 = f32[240,5,2880]{2,1,0:T(8,128)} dynamic-update-slice(f32[240,5,2880]{2,1,0:T(8,128)} %dynamic_update_slice.26, f32[240,5,360]{2,1,0:T(8,128)} %copy.94, s32[]{:T(128)} %constant.139.clone.1, s32[]{:T(128)} %constant.139.clone.1, s32[]{:T(128)S(6)} %select_n.195) | dynamic-update-slice | bytes 3456004 | tf_op jit(solution)/shard_map/dynamic_update_slice | solution.py:17
  447.6 3.9 copy.95
  451.4 42.1 %dynamic_update_slice.28 = f32[240,5,2880]{2,1,0:T(8,128)} dynamic-update-slice(f32[240,5,2880]{2,1,0:T(8,128)} %dynamic_update_slice.27, f32[240,5,360]{2,1,0:T(8,128)} %copy.95, s32[]{:T(128)} %constant.139.clone.1, s32[]{:T(128)} %constant.139.clone.1, s32[]{:T(128)S(6)} %select_n.197) | dynamic-update-slice | bytes 3456004 | tf_op jit(solution)/shard_map/dynamic_update_slice | solution.py:17
  493.5 3.9 copy.96
  497.4 42.1 %dynamic_update_slice.29 = f32[240,5,2880]{2,1,0:T(8,128)} dynamic-update-slice(f32[240,5,2880]{2,1,0:T(8,128)} %dynamic_update_slice.28, f32[240,5,360]{2,1,0:T(8,128)} %copy.96, s32[]{:T(128)} %constant.139.clone.1, s32[]{:T(128)} %constant.139.clone.1, s32[]{:T(128)S(6)} %select_n.199) | dynamic-update-slice | bytes 3456004 | tf_op jit(solution)/shard_map/dynamic_update_slice | solution.py:17
  539.5 3.9 copy.97
  543.3 42.3 %dynamic_update_slice.30 = f32[240,5,2880]{2,1,0:T(8,128)} dynamic-update-slice(f32[240,5,2880]{2,1,0:T(8,128)} %dynamic_update_slice.29, f32[240,5,360]{2,1,0:T(8,128)} %copy.97, s32[]{:T(128)} %constant.139.clone.1, s32[]{:T(128)} %constant.139.clone.1, s32[]{:T(128)S(6)} %select_n.201) | dynamic-update-slice | bytes 3456004 | tf_op jit(solution)/shard_map/dynamic_update_slice | solution.py:17
  585.6 3.9 copy.98
  589.5 42.1 %dynamic_update_slice.31 = f32[240,5,2880]{2,1,0:T(8,128)} dynamic-update-slice(f32[240,5,2880]{2,1,0:T(8,128)} %dynamic_update_slice.30, f32[240,5,360]{2,1,0:T(8,128)} %copy.98, s32[]{:T(128)} %constant.139.clone.1, s32[]{:T(128)} %constant.139.clone.1, s32[]{:T(128)S(6)} %select_n.203) | dynamic-update-slice | bytes 3456004 | tf_op jit(solution)/shard_map/dynamic_update_slice | solution.py:17
  631.6 25.0 %multiply_bitcast_fusion.1 = (f32[1,240,5,2880]{3,2,1,0:T(8,128)}, f32[1,240,5,2880]{3,2,1,0:T(8,128)}) fusion(f32[240,5,2880]{2,1,0:T(8,128)} %dynamic_update_slice.31, f32[240,2880]{1,0:T(8,128)} %get-tuple-element.17, f32[240,2880]{1,0:T(8,128)} %get-tuple-element.18), kind=kLoop, calls=%fused_computation.4 | loop fusion | flops 6912000 | bytes 47001600 | tf_op jit(solution)/shard_map/stack | solution.py:61
  656.5 32.8 %pad_maximum_fusion = f32[2,240,5,2880]{3,2,1,0:T(8,128)} fusion(f32[1,240,5,2880]{3,2,1,0:T(8,128)} %get-tuple-element.8, f32[1,240,5,2880]{3,2,1,0:T(8,128)} %get-tuple-element.7), kind=kLoop, calls=%fused_computation.2 | loop fusion | flops 6912000 | bytes 55296000 | tf_op jit(solution)/shard_map/stack | solution.py:61
  689.3 35.2 %reshape.271 = f32[2400,2880]{1,0:T(8,128)} reshape(f32[2,240,5,2880]{3,2,1,0:T(8,128)} %pad_maximum_fusion) | data formatting | bytes 55296000 | tf_op jit(solution)/shard_map/reshape | solution.py:62
  724.5 43.7 %fusion.6 = f32[2400,360]{0,1:T(8,128)S(1)} fusion(f32[2400,2880]{1,0:T(8,128)} %reshape.271, f32[2880,360]{1,0:T(8,128)} %fusion.66), kind=kOutput, calls=%fused_computation.13 | convolution fusion | flops 29859840000 | bytes 35251200 | tf_op jit(solution)/shard_map/dot_general | solution.py:64
  768.2 2.4 fusion.61
  770.6 2.8 copy.100
  773.4 3.1 squeeze.13
  776.5 2.8 copy.99
  779.3 3.1 squeeze.12
  782.4 5.0 fusion.13
  787.7 44.3 %all_to_all.11 = f32[4,60,5,360]{3,1,2,0:T(8,128)S(1)} all-to-all(f32[4,60,5,360]{3,1,2,0:T(8,128)S(1)} %copy.102), channel_id=1, replica_groups=mesh['lat'=4,'lon'=8] {'lat'}, dimensions={0} | all-to-all | bytes 3456000 | tf_op jit(solution)/shard_map/all_to_all | solution.py:153
  832.0 2.7 copy.106
  834.7 21.5 %scatter_fusion = f32[5,240,360]{2,0,1:T(8,128)S(1)} fusion(f32[5,240,360]{2,0,1:T(8,128)S(1)} %copy-done, s32[240]{0:T(256)S(1)} %bitcast.30, f32[240,5,360]{2,1,0:T(8,128)} %bitcast.28), kind=kCustom, calls=%fused_computation.1 | custom fusion | bytes 5184960 | tf_op jit(solution)/shard_map/scatter | solution.py:162
  (91 shorter events, 33.2 us)
Async XLA Ops:
  0.0 2.3 copy-start.6
  2.3 7.2 copy-start.1
  2.3 7.2 copy-start.2
  2.6 8.2 copy-start.4
  3.2 33.8 %collective-permute-start.3 = (f32[6,1,360]{2,0,1:T(8,128)}, f32[6,1,360]{2,0,1:T(8,128)S(1)}, u32[]{:S(2)}, u32[]{:S(2)}) collective-permute-start(f32[6,1,360]{2,0,1:T(8,128)} %get-tuple-element.12), channel_id=1, source_target_pairs={{0,8},{8,16},{16,24},{1,9},{9,17},{17,25},{2,10},{10,18},{18,26},{... | collective-permute-start | bytes 25928 | tf_op jit(solution)/shard_map/ppermute | solution.py:31
  8.2 29.7 %collective-permute-start.2 = (f32[6,1,360]{2,0,1:T(8,128)S(1)}, f32[6,1,360]{2,0,1:T(8,128)S(1)}, u32[]{:S(2)}, u32[]{:S(2)}) collective-permute-start(f32[6,1,360]{2,0,1:T(8,128)S(1)} %get-tuple-element.11), channel_id=1, source_target_pairs={{8,0},{16,8},{24,16},{9,1},{17,9},{25,17},{10,2},{18,10},{26,18},{... | collective-permute-start | bytes 25928 | tf_op jit(solution)/shard_map/ppermute | solution.py:33
  12.8 12.6 %collective-permute-start.1 = (f32[6,240,1]{1,2,0:T(1,128)}, f32[6,240,1]{1,2,0:T(1,128)}, u32[]{:S(2)}, u32[]{:S(2)}) collective-permute-start(f32[6,240,1]{1,2,0:T(1,128)} %copy.82), channel_id=1, source_target_pairs={{0,1},{1,2},{2,3},{3,4},{4,5},{5,6},{6,7},{7,0},{8,9},{9,10},{10,1... | collective-permute-start | bytes 17288 | tf_op jit(solution)/shard_map/ppermute | solution.py:31
  14.2 16.6 %collective-permute-start = (f32[6,240,1]{1,2,0:T(1,128)S(1)}, f32[6,240,1]{1,2,0:T(1,128)}, u32[]{:S(2)}, u32[]{:S(2)}) collective-permute-start(f32[6,240,1]{1,2,0:T(1,128)S(1)} %copy.80), channel_id=1, source_target_pairs={{1,0},{2,1},{3,2},{4,3},{5,4},{6,5},{7,6},{0,7},{9,8},{10,9},{11,1... | collective-permute-start | bytes 17288 | tf_op jit(solution)/shard_map/ppermute | solution.py:33
  32.6 4.4 copy-start.5
  37.0 1.0 copy-start.7
  37.0 1.0 copy-start.13
  37.0 1.0 copy-start.14
  37.0 1.0 copy-start.17
  43.0 2.6 copy-start.18
  43.1 2.6 copy-start.19
  99.1 127.0 %copy-start.15 = (s32[960]{0:T(1024)S(1)}, s32[960]{0:T(1024)}, u32[]{:S(2)}) copy-start(s32[960]{0:T(1024)} %param.9) | copy-start | bytes 11524
  99.1 127.4 %copy-start.16 = (f32[960]{0:T(1024)S(1)}, f32[960]{0:T(1024)}, u32[]{:S(2)}) copy-start(f32[960]{0:T(1024)} %param.10) | copy-start | bytes 11524
  101.7 23.8 %collective-permute-start.4 = (f32[240,5,360]{2,0,1:T(8,128)}, f32[240,5,360]{2,0,1:T(8,128)S(1)}, u32[]{:S(2)}, u32[]{:S(2)}) collective-permute-start(f32[240,5,360]{2,0,1:T(8,128)} %reshape.270), channel_id=1, source_target_pairs={{0,1},{1,2},{2,3},{3,4},{4,5},{5,6},{6,7},{7,0},{8,9},{9,10},{10,1... | collective-permute-start | bytes 5184008 | tf_op jit(solution)/shard_map/ppermute | solution.py:19
  125.6 1.3 copy-start.8
  126.9 23.6 %collective-permute-start.5 = (f32[240,5,360]{2,0,1:T(8,128)S(1)}, f32[240,5,360]{2,0,1:T(8,128)S(1)}, u32[]{:S(2)}, u32[]{:S(2)}) collective-permute-start(f32[240,5,360]{2,0,1:T(8,128)S(1)} %collective-permute-done.4), channel_id=1, source_target_pairs={{0,1},{1,2},{2,3},{3,4},{4,5},{5,6},{6,7},{7,0},{8,9},{9,10},{10,1... | collective-permute-start | bytes 5184008 | tf_op jit(solution)/shard_map/ppermute | solution.py:19
  150.5 1.3 copy-start.9
  151.8 23.6 %collective-permute-start.6 = (f32[240,5,360]{2,0,1:T(8,128)S(1)}, f32[240,5,360]{2,0,1:T(8,128)S(1)}, u32[]{:S(2)}, u32[]{:S(2)}) collective-permute-start(f32[240,5,360]{2,0,1:T(8,128)S(1)} %collective-permute-done.5), channel_id=1, source_target_pairs={{0,1},{1,2},{2,3},{3,4},{4,5},{5,6},{6,7},{7,0},{8,9},{9,10},{10,1... | collective-permute-start | bytes 5184008 | tf_op jit(solution)/shard_map/ppermute | solution.py:19
  175.4 1.2 copy-start.10
  176.7 23.6 %collective-permute-start.7 = (f32[240,5,360]{2,0,1:T(8,128)S(1)}, f32[240,5,360]{2,0,1:T(8,128)S(1)}, u32[]{:S(2)}, u32[]{:S(2)}) collective-permute-start(f32[240,5,360]{2,0,1:T(8,128)S(1)} %collective-permute-done.6), channel_id=1, source_target_pairs={{0,1},{1,2},{2,3},{3,4},{4,5},{5,6},{6,7},{7,0},{8,9},{9,10},{10,1... | collective-permute-start | bytes 5184008 | tf_op jit(solution)/shard_map/ppermute | solution.py:19
  200.3 1.2 copy-start.11
  201.5 23.7 %collective-permute-start.8 = (f32[240,5,360]{2,0,1:T(8,128)S(1)}, f32[240,5,360]{2,0,1:T(8,128)}, u32[]{:S(2)}, u32[]{:S(2)}) collective-permute-start(f32[240,5,360]{2,0,1:T(8,128)S(1)} %collective-permute-done.7), channel_id=1, source_target_pairs={{0,1},{1,2},{2,3},{3,4},{4,5},{5,6},{6,7},{7,0},{8,9},{9,10},{10,1... | collective-permute-start | bytes 5184008 | tf_op jit(solution)/shard_map/ppermute | solution.py:19
  225.3 24.0 %collective-permute-start.9 = (f32[240,5,360]{2,0,1:T(8,128)}, f32[240,5,360]{2,0,1:T(8,128)}, u32[]{:S(2)}, u32[]{:S(2)}) collective-permute-start(f32[240,5,360]{2,0,1:T(8,128)} %collective-permute-done.8), channel_id=1, source_target_pairs={{0,1},{1,2},{2,3},{3,4},{4,5},{5,6},{6,7},{7,0},{8,9},{9,10},{10,1... | collective-permute-start | bytes 5184008 | tf_op jit(solution)/shard_map/ppermute | solution.py:19
  249.2 336.4 %collective-permute-start.10 = (f32[240,5,360]{2,0,1:T(8,128)}, f32[240,5,360]{2,0,1:T(8,128)}, u32[]{:S(2)}, u32[]{:S(2)}) collective-permute-start(f32[240,5,360]{2,0,1:T(8,128)} %collective-permute-done.9), channel_id=1, source_target_pairs={{0,1},{1,2},{2,3},{3,4},{4,5},{5,6},{6,7},{7,0},{8,9},{9,10},{10,1... | collective-permute-start | bytes 5184008 | tf_op jit(solution)/shard_map/ppermute | solution.py:19
  263.5 18.3 %copy-start.3 = (f32[240,5,360]{2,0,1:T(8,128)S(1)}, f32[240,5,360]{2,0,1:T(8,128)}, u32[]{:S(2)}) copy-start(f32[240,5,360]{2,0,1:T(8,128)} %reshape.270) | copy-start | bytes 5184004
  832.0 2.7 copy-start
  832.0 2.7 copy-start.12
